TPU v7x, 32 devices: a whole 2x2x4 slice. The times are simulated.
32 devices in a mesh: gx: 4 (over x, core), gy: 4 (over z), gz: 2 (over y).
Axes of the slice: x: 2, y: 2, z: 4, core: 2. Of those that a mesh axis runs over, the one named last changes fastest.
Arguments:
- right_side: float32 [64, 32, 256], P('gx', 'gy', 'gz'), may hold values from -6 to 6
- inv_density: float32 [64, 32, 256], P('gx', 'gy', 'gz'), may hold values from 0.25 to 4
Outputs:
- pressure: float32 [64, 32, 256], P('gx', 'gy', 'gz')
- residual: float32 [64, 32, 256], P('gx', 'gy', 'gz')
All inputs are finite; a program needn't handle non-finite values.
Results may differ from a plain program's by a relative error of at most 0.0003.
Values sent between devices are 32-bit elements; how exact they have to be, the bound alone decides.
A program may use at most 64 MiB of HBM per device.

v0:
```python
import jax
import jax.numpy as jnp
from jax import lax
from jax.sharding import PartitionSpec as P

LEVELS = 3
DEGREE = 2
COARSE_DEGREE = 6


def extended(cells, sides, width):
    for axis, dim in sides:
        count = lax.axis_size(axis)
        ends = count - 1
        head = lax.slice_in_dim(cells, 0, width, axis=dim)
        tail = lax.slice_in_dim(cells, cells.shape[dim] - width, cells.shape[dim], axis=dim)
        cells = jnp.concatenate(
            [
                lax.ppermute(tail, axis, [(i, (i + 1) % count) for i in range(ends)]),
                cells,
                lax.ppermute(head, axis, [((i + 1) % count, i) for i in range(ends)]),
            ],
            axis=dim,
        )
    return cells


def mean_cells(field):
    n, m, k = field.shape
    return field.reshape(n // 2, 2, m // 2, 2, k // 2, 2).sum(axis=(1, 3, 5)) * 0.125


def copy_cells(field):
    return jnp.repeat(jnp.repeat(jnp.repeat(field, 2, 0), 2, 1), 2, 2)


def harmonic(first, second):
    inside = first * second > 0.0
    return jnp.where(inside, 2.0 * first * second / (first + second), first + second)


def face_coefs(padded):
    face_x = harmonic(padded[:-1, 1:-1, 1:-1], padded[1:, 1:-1, 1:-1])
    face_y = harmonic(padded[1:-1, :-1, 1:-1], padded[1:-1, 1:, 1:-1])
    face_z = harmonic(padded[1:-1, 1:-1, :-1], padded[1:-1, 1:-1, 1:])
    return (face_x, face_y, face_z)


def operate(padded, faces, scale):
    face_x, face_y, face_z = faces
    center = padded[1:-1, 1:-1, 1:-1]
    total = face_x[1:] * (center - padded[2:, 1:-1, 1:-1])
    total = total + face_x[:-1] * (center - padded[:-2, 1:-1, 1:-1])
    total = total + face_y[:, 1:] * (center - padded[1:-1, 2:, 1:-1])
    total = total + face_y[:, :-1] * (center - padded[1:-1, :-2, 1:-1])
    total = total + face_z[:, :, 1:] * (center - padded[1:-1, 1:-1, 2:])
    total = total + face_z[:, :, :-1] * (center - padded[1:-1, 1:-1, :-2])
    return scale * total


def face_total(faces):
    face_x, face_y, face_z = faces
    return (
        face_x[1:]
        + face_x[:-1]
        + face_y[:, 1:]
        + face_y[:, :-1]
        + face_z[:, :, 1:]
        + face_z[:, :, :-1]
    )


def inverse_diag(faces, scale):
    return 1.0 / (scale * face_total(faces))


def chebyshev(start, source, steps, lower, upper, apply_op, inv_diag):
    theta = (upper + lower) / 2.0
    delta = (upper - lower) / 2.0
    sigma = theta / delta
    rho_now = 1.0 / sigma
    if start is None:
        remain = source
        solution = jnp.zeros_like(source)
    else:
        remain = source - apply_op(start)
        solution = start
    update = remain * inv_diag / theta
    solution = solution + update
    for index in range(steps - 1):
        rho_next = 1.0 / (2.0 * sigma - rho_now)
        remain = source - apply_op(solution)
        update = rho_next * rho_now * update + 2.0 * rho_next / delta * (remain * inv_diag)
        solution = solution + update
        rho_now = rho_next
    return solution


def field_spread(field):
    return extended(field, (("gx", 0), ("gy", 1), ("gz", 2)), 1)


def coef_spread(coef):
    return extended(coef, (("gx", 0), ("gy", 1), ("gz", 2)), 1)


def coarse_solve(source, coef, pad_field, pad_coef):
    scale = 0.25**LEVELS
    faces = face_coefs(pad_coef(coef))
    inv_diag = inverse_diag(faces, scale)

    def apply_op(field):
        return operate(pad_field(field), faces, scale)

    return chebyshev(None, source, COARSE_DEGREE, 0.05, 2.0, apply_op, inv_diag)


def coarsest(source, coef):
    return coarse_solve(source, coef, field_spread, coef_spread)


def vcycle(depth, source, coef):
    if depth == LEVELS:
        return (coarsest(source, coef), None)
    scale = 0.25**depth
    faces = face_coefs(coef_spread(coef))
    inv_diag = inverse_diag(faces, scale)

    def apply_op(field):
        return operate(field_spread(field), faces, scale)

    solution = chebyshev(None, source, DEGREE, 0.3, 2.0, apply_op, inv_diag)
    remain = source - apply_op(solution)
    correction, unused = vcycle(depth + 1, mean_cells(remain), mean_cells(coef))
    solution = solution + copy_cells(correction)
    solution = chebyshev(solution, source, DEGREE, 0.3, 2.0, apply_op, inv_diag)
    return (solution, apply_op)


def per_device(right_side, inv_density):
    pressure, apply_op = vcycle(0, right_side, inv_density)
    return (pressure, right_side - apply_op(pressure))


def solution(mesh):
    in_specs = (P("gx", "gy", "gz"), P("gx", "gy", "gz"))
    out_specs = (P("gx", "gy", "gz"), P("gx", "gy", "gz"))
    return jax.shard_map(
        per_device, mesh=mesh, in_specs=in_specs, out_specs=out_specs, check_vma=False
    )
```

profile of v0, /device:TPU:0, one launch (start us, length us, event | category | flops | bytes accessed | tf_op | source)
XLA Modules:
  0.0 493.5 jit_solution(11075347509136898638)
XLA Ops:
  5.8 6.3 %reshape.236 = f32[8,2,4,2,64,2]{5,4,3,2,1,0:T(8,128)} reshape(f32[16,8,128]{2,1,0:T(8,128)} %param.3) | data formatting | bytes 131072 | tf_op jit(solution)/shard_map/reshape | solution.py:30
  14.7 4.5 collective-permute-start.18
  33.4 5.2 %collective-permute-start.2 = (f32[18,1,128]{2,1,0:T(1,128)S(1)}, f32[18,1,128]{2,1,0:T(1,128)S(1)}, u32[]{:S(2)}, u32[]{:S(2)}) collective-permute-start(f32[18,1,128]{2,1,0:T(1,128)S(1)} %get-tuple-element.67), channel_id=1, source_target_pairs={{0,2},{2,4},{4,6},{1,3},{3,5},{5,7},{8,10},{10,12},{12,14},{9,11},... | collective-permute-start | bytes 27656 | tf_op jit(solution)/shard_map/ppermute | solution.py:19
  47.0 4.4 collective-permute-start.56
  60.3 4.5 collective-permute-start.9
  67.5 4.5 collective-permute-done.8
  73.4 4.6 collective-permute-start.11
  85.5 4.5 collective-permute-start.22
  96.5 4.5 collective-permute-done.14
  102.4 4.6 collective-permute-start.17
  109.6 5.6 %reshape.235 = f32[8,2,4,2,64,2]{5,4,3,2,1,0:T(8,128)} reshape(f32[16,8,128]{2,1,0:T(8,128)S(1)} %fusion.57) | data formatting | bytes 131072 | tf_op jit(solution)/shard_map/reshape | solution.py:30
  122.8 3.9 collective-permute-start.38
  129.4 3.9 collective-permute-start.27
  140.2 4.5 collective-permute-start.29
  151.8 4.4 collective-permute-done.30
  159.8 4.2 collective-permute-start.40
  165.5 4.5 collective-permute-start.35
  179.9 4.6 collective-permute-start.45
  187.1 4.5 collective-permute-start.58
  193.1 4.5 collective-permute-start.47
  206.0 4.6 collective-permute-start.51
  212.0 4.1 collective-permute-done.50
  217.5 4.5 collective-permute-start.53
  230.7 3.9 collective-permute-start.63
  235.9 4.2 collective-permute-done.62
  241.5 4.5 collective-permute-start.65
  257.6 4.2 collective-permute-done.68
  263.1 4.5 collective-permute-start.71
  279.2 4.2 collective-permute-done.74
  284.7 4.5 collective-permute-start.77
  300.8 4.2 collective-permute-done.80
  306.3 4.7 collective-permute-start.83
  322.6 4.2 collective-permute-done.86
  328.1 4.5 collective-permute-start.89
  344.4 4.2 collective-permute-done.92
  350.0 4.5 collective-permute-start.95
  366.2 4.2 collective-permute-done.98
  371.7 4.5 collective-permute-start.101
  388.2 4.2 collective-permute-done.104
  393.8 4.5 collective-permute-start.107
  410.3 4.2 collective-permute-done.110
  415.9 4.5 collective-permute-start.113
  432.9 4.2 collective-permute-done.116
  438.5 4.6 collective-permute-start.119
  456.0 4.2 collective-permute-done.122
  461.6 4.6 collective-permute-start.125
  479.0 4.2 collective-permute-done.128
  484.6 4.6 collective-permute-start.131
  (416 shorter events, 276.3 us)
Async XLA Ops:
  1.3 30.7 %collective-permute-start.1 = (f32[1,8,128]{2,1,0:T(8,128)S(1)}, f32[1,8,128]{2,1,0:T(8,128)S(1)}, u32[]{:S(2)}, u32[]{:S(2)}) collective-permute-start(f32[1,8,128]{2,1,0:T(8,128)S(1)} %get-tuple-element.81), channel_id=1, source_target_pairs={{8,0},{16,8},{24,16},{9,1},{17,9},{25,17},{10,2},{18,10},{26,18},{... | collective-permute-start | bytes 12296 | tf_op jit(solution)/shard_map/ppermute | solution.py:21
  2.6 29.4 %collective-permute-start = (f32[1,8,128]{2,1,0:T(8,128)S(1)}, f32[1,8,128]{2,1,0:T(8,128)S(1)}, u32[]{:S(2)}, u32[]{:S(2)}) collective-permute-start(f32[1,8,128]{2,1,0:T(8,128)S(1)} %get-tuple-element.82), channel_id=1, source_target_pairs={{0,8},{8,16},{16,24},{1,9},{9,17},{17,25},{2,10},{10,18},{18,26},{... | collective-permute-start | bytes 12296 | tf_op jit(solution)/shard_map/ppermute | solution.py:19
  14.7 39.2 %collective-permute-start.18 = (f32[1,4,64]{2,1,0:T(4,128)S(1)}, f32[1,4,64]{2,1,0:T(4,128)S(1)}, u32[]{:S(2)}, u32[]{:S(2)}) collective-permute-start(f32[1,4,64]{2,1,0:T(4,128)S(1)} %get-tuple-element.121), channel_id=1, source_target_pairs={{0,8},{8,16},{16,24},{1,9},{9,17},{17,25},{2,10},{10,18},{18,26},{... | collective-permute-start | bytes 3080 | tf_op jit(solution)/shard_map/ppermute | solution.py:19
  28.2 27.0 %collective-permute-start.19 = (f32[1,4,64]{2,1,0:T(4,128)S(1)}, f32[1,4,64]{2,1,0:T(4,128)S(1)}, u32[]{:S(2)}, u32[]{:S(2)}) collective-permute-start(f32[1,4,64]{2,1,0:T(4,128)S(1)} %get-tuple-element.122), channel_id=1, source_target_pairs={{8,0},{16,8},{24,16},{9,1},{17,9},{25,17},{10,2},{18,10},{26,18},{... | collective-permute-start | bytes 3080 | tf_op jit(solution)/shard_map/ppermute | solution.py:21
  30.7 145.8 %collective-permute-start.57 = (f32[4,1,16]{2,0,1:T(4,128)S(1)}, f32[4,1,16]{2,0,1:T(4,128)S(1)}, u32[]{:S(2)}, u32[]{:S(2)}) collective-permute-start(f32[4,1,16]{2,0,1:T(4,128)S(1)} %pad_maximum_fusion.283), channel_id=1, source_target_pairs={{2,0},{4,2},{6,4},{3,1},{5,3},{7,5},{10,8},{12,10},{14,12},{11,9},... | collective-permute-start | bytes 776 | tf_op jit(solution)/shard_map/ppermute | solution.py:21
  32.1 7.9 %collective-permute-start.3 = (f32[18,1,128]{2,1,0:T(1,128)S(1)}, f32[18,1,128]{2,1,0:T(1,128)S(1)}, u32[]{:S(2)}, u32[]{:S(2)}) collective-permute-start(f32[18,1,128]{2,1,0:T(1,128)S(1)} %get-tuple-element.66), channel_id=1, source_target_pairs={{2,0},{4,2},{6,4},{3,1},{5,3},{7,5},{10,8},{12,10},{14,12},{11,9},... | collective-permute-start | bytes 27656 | tf_op jit(solution)/shard_map/ppermute | solution.py:21
  33.4 6.5 %collective-permute-start.2 = (f32[18,1,128]{2,1,0:T(1,128)S(1)}, f32[18,1,128]{2,1,0:T(1,128)S(1)}, u32[]{:S(2)}, u32[]{:S(2)}) collective-permute-start(f32[18,1,128]{2,1,0:T(1,128)S(1)} %get-tuple-element.67), channel_id=1, source_target_pairs={{0,2},{2,4},{4,6},{1,3},{3,5},{5,7},{8,10},{10,12},{12,14},{9,11},... | collective-permute-start | bytes 27656 | tf_op jit(solution)/shard_map/ppermute | solution.py:19
  40.1 6.9 %collective-permute-start.4 = (f32[18,10,1]{2,0,1:T(8,128)S(1)}, f32[18,10,1]{2,0,1:T(8,128)S(1)}, u32[]{:S(2)}, u32[]{:S(2)}) collective-permute-start(f32[18,10,1]{2,0,1:T(8,128)S(1)} %get-tuple-element.54), channel_id=1, source_target_pairs={{0,1},{2,3},{4,5},{6,7},{8,9},{10,11},{12,13},{14,15},{16,17},{18,... | collective-permute-start | bytes 2168 | tf_op jit(solution)/shard_map/ppermute | solution.py:19
  43.5 8.0 %collective-permute-start.5 = (f32[18,10,1]{2,0,1:T(8,128)S(1)}, f32[18,10,1]{2,0,1:T(8,128)S(1)}, u32[]{:S(2)}, u32[]{:S(2)}) collective-permute-start(f32[18,10,1]{2,0,1:T(8,128)S(1)} %get-tuple-element.55), channel_id=1, source_target_pairs={{1,0},{3,2},{5,4},{7,6},{9,8},{11,10},{13,12},{15,14},{17,16},{19,... | collective-permute-start | bytes 2168 | tf_op jit(solution)/shard_map/ppermute | solution.py:21
  47.0 129.5 %collective-permute-start.56 = (f32[4,1,16]{2,0,1:T(4,128)S(1)}, f32[4,1,16]{2,0,1:T(4,128)S(1)}, u32[]{:S(2)}, u32[]{:S(2)}) collective-permute-start(f32[4,1,16]{2,0,1:T(4,128)S(1)} %pad_maximum_fusion.283), channel_id=1, source_target_pairs={{0,2},{2,4},{4,6},{1,3},{3,5},{5,7},{8,10},{10,12},{12,14},{9,11},... | collective-permute-start | bytes 776 | tf_op jit(solution)/shard_map/ppermute | solution.py:19
  52.0 6.9 %collective-permute-start.7 = (f32[1,8,128]{2,1,0:T(8,128)S(1)}, f32[1,8,128]{2,1,0:T(8,128)S(1)}, u32[]{:S(2)}, u32[]{:S(2)}) collective-permute-start(f32[1,8,128]{2,1,0:T(8,128)S(1)} %get-tuple-element.76), channel_id=1, source_target_pairs={{0,8},{8,16},{16,24},{1,9},{9,17},{17,25},{2,10},{10,18},{18,26},{... | collective-permute-start | bytes 12296 | tf_op jit(solution)/shard_map/ppermute | solution.py:19
  54.0 6.2 %collective-permute-start.6 = (f32[1,8,128]{2,1,0:T(8,128)S(1)}, f32[1,8,128]{2,1,0:T(8,128)S(1)}, u32[]{:S(2)}, u32[]{:S(2)}) collective-permute-start(f32[1,8,128]{2,1,0:T(8,128)S(1)} %get-tuple-element.77), channel_id=1, source_target_pairs={{8,0},{16,8},{24,16},{9,1},{17,9},{25,17},{10,2},{18,10},{26,18},{... | collective-permute-start | bytes 12296 | tf_op jit(solution)/shard_map/ppermute | solution.py:21
  55.3 18.1 %collective-permute-start.20 = (f32[10,1,64]{2,1,0:T(1,128)S(1)}, f32[10,1,64]{2,1,0:T(1,128)S(1)}, u32[]{:S(2)}, u32[]{:S(2)}) collective-permute-start(f32[10,1,64]{2,1,0:T(1,128)S(1)} %get-tuple-element.101), channel_id=1, source_target_pairs={{0,2},{2,4},{4,6},{1,3},{3,5},{5,7},{8,10},{10,12},{12,14},{9,11},... | collective-permute-start | bytes 7688 | tf_op jit(solution)/shard_map/ppermute | solution.py:19
  58.9 19.1 %collective-permute-start.21 = (f32[10,1,64]{2,1,0:T(1,128)S(1)}, f32[10,1,64]{2,1,0:T(1,128)S(1)}, u32[]{:S(2)}, u32[]{:S(2)}) collective-permute-start(f32[10,1,64]{2,1,0:T(1,128)S(1)} %get-tuple-element.102), channel_id=1, source_target_pairs={{2,0},{4,2},{6,4},{3,1},{5,3},{7,5},{10,8},{12,10},{14,12},{11,9},... | collective-permute-start | bytes 7688 | tf_op jit(solution)/shard_map/ppermute | solution.py:21
  72.1 7.8 %collective-permute-start.10 = (f32[18,10,1]{2,0,1:T(8,128)S(1)}, f32[18,10,1]{2,0,1:T(8,128)S(1)}, u32[]{:S(2)}, u32[]{:S(2)}) collective-permute-start(f32[18,10,1]{2,0,1:T(8,128)S(1)} %get-tuple-element.50), channel_id=1, source_target_pairs={{1,0},{3,2},{5,4},{7,6},{9,8},{11,10},{13,12},{15,14},{17,16},{19,... | collective-permute-start | bytes 2168 | tf_op jit(solution)/shard_map/ppermute | solution.py:21
  73.4 7.7 %collective-permute-start.11 = (f32[18,10,1]{2,0,1:T(8,128)S(1)}, f32[18,10,1]{2,0,1:T(8,128)S(1)}, u32[]{:S(2)}, u32[]{:S(2)}) collective-permute-start(f32[18,10,1]{2,0,1:T(8,128)S(1)} %get-tuple-element.51), channel_id=1, source_target_pairs={{0,1},{2,3},{4,5},{6,7},{8,9},{10,11},{12,13},{14,15},{16,17},{18,... | collective-permute-start | bytes 2168 | tf_op jit(solution)/shard_map/ppermute | solution.py:19
  82.8 7.2 %collective-permute-start.12 = (f32[1,8,128]{2,1,0:T(8,128)S(1)}, f32[1,8,128]{2,1,0:T(8,128)S(1)}, u32[]{:S(2)}, u32[]{:S(2)}) collective-permute-start(f32[1,8,128]{2,1,0:T(8,128)S(1)} %get-tuple-element.75), channel_id=1, source_target_pairs={{8,0},{16,8},{24,16},{9,1},{17,9},{25,17},{10,2},{18,10},{26,18},{... | collective-permute-start | bytes 12296 | tf_op jit(solution)/shard_map/ppermute | solution.py:21
  84.2 18.2 %collective-permute-start.23 = (f32[10,6,1]{2,1,0:T(8,128)S(1)}, f32[10,6,1]{2,1,0:T(8,128)S(1)}, u32[]{:S(2)}, u32[]{:S(2)}) collective-permute-start(f32[10,6,1]{2,1,0:T(8,128)S(1)} %get-tuple-element.91), channel_id=1, source_target_pairs={{1,0},{3,2},{5,4},{7,6},{9,8},{11,10},{13,12},{15,14},{17,16},{19,... | collective-permute-start | bytes 728 | tf_op jit(solution)/shard_map/ppermute | solution.py:21
  85.5 21.4 %collective-permute-start.22 = (f32[10,6,1]{2,1,0:T(8,128)S(1)}, f32[10,6,1]{2,1,0:T(8,128)S(1)}, u32[]{:S(2)}, u32[]{:S(2)}) collective-permute-start(f32[10,6,1]{2,1,0:T(8,128)S(1)} %get-tuple-element.92), channel_id=1, source_target_pairs={{0,1},{2,3},{4,5},{6,7},{8,9},{10,11},{12,13},{14,15},{16,17},{18,... | collective-permute-start | bytes 728 | tf_op jit(solution)/shard_map/ppermute | solution.py:19
  101.1 6.8 %collective-permute-start.16 = (f32[18,10,1]{2,0,1:T(8,128)S(1)}, f32[18,10,1]{2,0,1:T(8,128)S(1)}, u32[]{:S(2)}, u32[]{:S(2)}) collective-permute-start(f32[18,10,1]{2,0,1:T(8,128)S(1)} %get-tuple-element.46), channel_id=1, source_target_pairs={{1,0},{3,2},{5,4},{7,6},{9,8},{11,10},{13,12},{15,14},{17,16},{19,... | collective-permute-start | bytes 2168 | tf_op jit(solution)/shard_map/ppermute | solution.py:21
  102.4 7.0 %collective-permute-start.17 = (f32[18,10,1]{2,0,1:T(8,128)S(1)}, f32[18,10,1]{2,0,1:T(8,128)S(1)}, u32[]{:S(2)}, u32[]{:S(2)}) collective-permute-start(f32[18,10,1]{2,0,1:T(8,128)S(1)} %get-tuple-element.47), channel_id=1, source_target_pairs={{0,1},{2,3},{4,5},{6,7},{8,9},{10,11},{12,13},{14,15},{16,17},{18,... | collective-permute-start | bytes 2168 | tf_op jit(solution)/shard_map/ppermute | solution.py:19
  117.8 8.8 %collective-permute-start.25 = (f32[1,4,64]{2,1,0:T(4,128)S(1)}, f32[1,4,64]{2,1,0:T(4,128)S(1)}, u32[]{:S(2)}, u32[]{:S(2)}) collective-permute-start(f32[1,4,64]{2,1,0:T(4,128)S(1)} %get-tuple-element.119), channel_id=1, source_target_pairs={{0,8},{8,16},{16,24},{1,9},{9,17},{17,25},{2,10},{10,18},{18,26},{... | collective-permute-start | bytes 3080 | tf_op jit(solution)/shard_map/ppermute | solution.py:19
  121.5 7.9 %collective-permute-start.24 = (f32[1,4,64]{2,1,0:T(4,128)S(1)}, f32[1,4,64]{2,1,0:T(4,128)S(1)}, u32[]{:S(2)}, u32[]{:S(2)}) collective-permute-start(f32[1,4,64]{2,1,0:T(4,128)S(1)} %get-tuple-element.120), channel_id=1, source_target_pairs={{8,0},{16,8},{24,16},{9,1},{17,9},{25,17},{10,2},{18,10},{26,18},{... | collective-permute-start | bytes 3080 | tf_op jit(solution)/shard_map/ppermute | solution.py:21
  122.8 17.5 %collective-permute-start.38 = (f32[6,1,32]{2,0,1:T(8,128)S(1)}, f32[6,1,32]{2,0,1:T(8,128)S(1)}, u32[]{:S(2)}, u32[]{:S(2)}) collective-permute-start(f32[6,1,32]{2,0,1:T(8,128)S(1)} %get-tuple-element.131), channel_id=1, source_target_pairs={{0,2},{2,4},{4,6},{1,3},{3,5},{5,7},{8,10},{10,12},{12,14},{9,11},... | collective-permute-start | bytes 2312 | tf_op jit(solution)/shard_map/ppermute | solution.py:19
  134.7 10.1 %collective-permute-start.39 = (f32[6,1,32]{2,0,1:T(8,128)S(1)}, f32[6,1,32]{2,0,1:T(8,128)S(1)}, u32[]{:S(2)}, u32[]{:S(2)}) collective-permute-start(f32[6,1,32]{2,0,1:T(8,128)S(1)} %get-tuple-element.132), channel_id=1, source_target_pairs={{2,0},{4,2},{6,4},{3,1},{5,3},{7,5},{10,8},{12,10},{14,12},{11,9},... | collective-permute-start | bytes 2312 | tf_op jit(solution)/shard_map/ppermute | solution.py:21
  140.2 6.2 %collective-permute-start.29 = (f32[10,6,1]{2,1,0:T(8,128)S(1)}, f32[10,6,1]{2,1,0:T(8,128)S(1)}, u32[]{:S(2)}, u32[]{:S(2)}) collective-permute-start(f32[10,6,1]{2,1,0:T(8,128)S(1)} %get-tuple-element.90), channel_id=1, source_target_pairs={{0,1},{2,3},{4,5},{6,7},{8,9},{10,11},{12,13},{14,15},{16,17},{18,... | collective-permute-start | bytes 728 | tf_op jit(solution)/shard_map/ppermute | solution.py:19
  149.1 7.1 %collective-permute-start.30 = (f32[1,4,64]{2,1,0:T(4,128)S(1)}, f32[1,4,64]{2,1,0:T(4,128)S(1)}, u32[]{:S(2)}, u32[]{:S(2)}) collective-permute-start(f32[1,4,64]{2,1,0:T(4,128)S(1)} %get-tuple-element.118), channel_id=1, source_target_pairs={{8,0},{16,8},{24,16},{9,1},{17,9},{25,17},{10,2},{18,10},{26,18},{... | collective-permute-start | bytes 3080 | tf_op jit(solution)/shard_map/ppermute | solution.py:21
  150.5 15.0 %collective-permute-start.41 = (f32[6,4,1]{2,0,1:T(8,128)S(1)}, f32[6,4,1]{2,0,1:T(8,128)S(1)}, u32[]{:S(2)}, u32[]{:S(2)}) collective-permute-start(f32[6,4,1]{2,0,1:T(8,128)S(1)} %get-tuple-element.115), channel_id=1, source_target_pairs={{1,0},{3,2},{5,4},{7,6},{9,8},{11,10},{13,12},{15,14},{17,16},{19,... | collective-permute-start | bytes 296 | tf_op jit(solution)/shard_map/ppermute | solution.py:21
  159.8 10.2 %collective-permute-start.40 = (f32[6,4,1]{2,0,1:T(8,128)S(1)}, f32[6,4,1]{2,0,1:T(8,128)S(1)}, u32[]{:S(2)}, u32[]{:S(2)}) collective-permute-start(f32[6,4,1]{2,0,1:T(8,128)S(1)} %get-tuple-element.116), channel_id=1, source_target_pairs={{0,1},{2,3},{4,5},{6,7},{8,9},{10,11},{12,13},{14,15},{16,17},{18,... | collective-permute-start | bytes 296 | tf_op jit(solution)/shard_map/ppermute | solution.py:19
  165.5 6.2 %collective-permute-start.35 = (f32[10,6,1]{2,1,0:T(8,128)S(1)}, f32[10,6,1]{2,1,0:T(8,128)S(1)}, u32[]{:S(2)}, u32[]{:S(2)}) collective-permute-start(f32[10,6,1]{2,1,0:T(8,128)S(1)} %get-tuple-element.88), channel_id=1, source_target_pairs={{0,1},{2,3},{4,5},{6,7},{8,9},{10,11},{12,13},{14,15},{16,17},{18,... | collective-permute-start | bytes 728 | tf_op jit(solution)/shard_map/ppermute | solution.py:19
  179.9 11.8 %collective-permute-start.45 = (f32[6,1,32]{2,0,1:T(8,128)S(1)}, f32[6,1,32]{2,0,1:T(8,128)S(1)}, u32[]{:S(2)}, u32[]{:S(2)}) collective-permute-start(f32[6,1,32]{2,0,1:T(8,128)S(1)} %get-tuple-element.129), channel_id=1, source_target_pairs={{0,2},{2,4},{4,6},{1,3},{3,5},{5,7},{8,10},{10,12},{12,14},{9,11},... | collective-permute-start | bytes 2312 | tf_op jit(solution)/shard_map/ppermute | solution.py:19
  184.5 7.2 %collective-permute-start.44 = (f32[6,1,32]{2,0,1:T(8,128)S(1)}, f32[6,1,32]{2,0,1:T(8,128)S(1)}, u32[]{:S(2)}, u32[]{:S(2)}) collective-permute-start(f32[6,1,32]{2,0,1:T(8,128)S(1)} %get-tuple-element.130), channel_id=1, source_target_pairs={{2,0},{4,2},{6,4},{3,1},{5,3},{7,5},{10,8},{12,10},{14,12},{11,9},... | collective-permute-start | bytes 2312 | tf_op jit(solution)/shard_map/ppermute | solution.py:21
  185.8 26.1 %collective-permute-start.59 = (f32[4,3,1]{2,0,1:T(4,128)S(1)}, f32[4,3,1]{2,0,1:T(4,128)S(1)}, u32[]{:S(2)}, u32[]{:S(2)}) collective-permute-start(f32[4,3,1]{2,0,1:T(4,128)S(1)} %get-tuple-element.143), channel_id=1, source_target_pairs={{1,0},{3,2},{5,4},{7,6},{9,8},{11,10},{13,12},{15,14},{17,16},{19,... | collective-permute-start | bytes 152 | tf_op jit(solution)/shard_map/ppermute | solution.py:21
  187.1 24.8 %collective-permute-start.58 = (f32[4,3,1]{2,0,1:T(4,128)S(1)}, f32[4,3,1]{2,0,1:T(4,128)S(1)}, u32[]{:S(2)}, u32[]{:S(2)}) collective-permute-start(f32[4,3,1]{2,0,1:T(4,128)S(1)} %get-tuple-element.144), channel_id=1, source_target_pairs={{0,1},{2,3},{4,5},{6,7},{8,9},{10,11},{12,13},{14,15},{16,17},{18,... | collective-permute-start | bytes 152 | tf_op jit(solution)/shard_map/ppermute | solution.py:19
  193.1 6.0 %collective-permute-start.47 = (f32[6,4,1]{2,0,1:T(8,128)S(1)}, f32[6,4,1]{2,0,1:T(8,128)S(1)}, u32[]{:S(2)}, u32[]{:S(2)}) collective-permute-start(f32[6,4,1]{2,0,1:T(8,128)S(1)} %get-tuple-element.114), channel_id=1, source_target_pairs={{0,1},{2,3},{4,5},{6,7},{8,9},{10,11},{12,13},{14,15},{16,17},{18,... | collective-permute-start | bytes 296 | tf_op jit(solution)/shard_map/ppermute | solution.py:19
  217.5 6.0 %collective-permute-start.53 = (f32[6,4,1]{2,0,1:T(8,128)S(1)}, f32[6,4,1]{2,0,1:T(8,128)S(1)}, u32[]{:S(2)}, u32[]{:S(2)}) collective-permute-start(f32[6,4,1]{2,0,1:T(8,128)S(1)} %get-tuple-element.112), channel_id=1, source_target_pairs={{0,1},{2,3},{4,5},{6,7},{8,9},{10,11},{12,13},{14,15},{16,17},{18,... | collective-permute-start | bytes 296 | tf_op jit(solution)/shard_map/ppermute | solution.py:19
  305.0 6.0 %collective-permute-start.82 = (f32[4,3,1]{2,0,1:T(4,128)S(1)}, f32[4,3,1]{2,0,1:T(4,128)S(1)}, u32[]{:S(2)}, u32[]{:S(2)}) collective-permute-start(f32[4,3,1]{2,0,1:T(4,128)S(1)} %get-tuple-element.135), channel_id=1, source_target_pairs={{1,0},{3,2},{5,4},{7,6},{9,8},{11,10},{13,12},{15,14},{17,16},{19,... | collective-permute-start | bytes 152 | tf_op jit(solution)/shard_map/ppermute | solution.py:21
  306.3 6.1 %collective-permute-start.83 = (f32[4,3,1]{2,0,1:T(4,128)S(1)}, f32[4,3,1]{2,0,1:T(4,128)S(1)}, u32[]{:S(2)}, u32[]{:S(2)}) collective-permute-start(f32[4,3,1]{2,0,1:T(4,128)S(1)} %get-tuple-element.136), channel_id=1, source_target_pairs={{0,1},{2,3},{4,5},{6,7},{8,9},{10,11},{12,13},{14,15},{16,17},{18,... | collective-permute-start | bytes 152 | tf_op jit(solution)/shard_map/ppermute | solution.py:19
  392.5 6.3 %collective-permute-start.106 = (f32[10,6,1]{2,1,0:T(8,128)S(1)}, f32[10,6,1]{2,1,0:T(8,128)S(1)}, u32[]{:S(2)}, u32[]{:S(2)}) collective-permute-start(f32[10,6,1]{2,1,0:T(8,128)S(1)} %get-tuple-element.85), channel_id=1, source_target_pairs={{1,0},{3,2},{5,4},{7,6},{9,8},{11,10},{13,12},{15,14},{17,16},{19,... | collective-permute-start | bytes 728 | tf_op jit(solution)/shard_map/ppermute | solution.py:21
  393.8 6.2 %collective-permute-start.107 = (f32[10,6,1]{2,1,0:T(8,128)S(1)}, f32[10,6,1]{2,1,0:T(8,128)S(1)}, u32[]{:S(2)}, u32[]{:S(2)}) collective-permute-start(f32[10,6,1]{2,1,0:T(8,128)S(1)} %get-tuple-element.86), channel_id=1, source_target_pairs={{0,1},{2,3},{4,5},{6,7},{8,9},{10,11},{12,13},{14,15},{16,17},{18,... | collective-permute-start | bytes 728 | tf_op jit(solution)/shard_map/ppermute | solution.py:19
  414.6 6.3 %collective-permute-start.112 = (f32[10,6,1]{2,1,0:T(8,128)S(1)}, f32[10,6,1]{2,1,0:T(8,128)S(1)}, u32[]{:S(2)}, u32[]{:S(2)}) collective-permute-start(f32[10,6,1]{2,1,0:T(8,128)S(1)} %get-tuple-element.83), channel_id=1, source_target_pairs={{1,0},{3,2},{5,4},{7,6},{9,8},{11,10},{13,12},{15,14},{17,16},{19,... | collective-permute-start | bytes 728 | tf_op jit(solution)/shard_map/ppermute | solution.py:21
  415.9 6.2 %collective-permute-start.113 = (f32[10,6,1]{2,1,0:T(8,128)S(1)}, f32[10,6,1]{2,1,0:T(8,128)S(1)}, u32[]{:S(2)}, u32[]{:S(2)}) collective-permute-start(f32[10,6,1]{2,1,0:T(8,128)S(1)} %get-tuple-element.84), channel_id=1, source_target_pairs={{0,1},{2,3},{4,5},{6,7},{8,9},{10,11},{12,13},{14,15},{16,17},{18,... | collective-permute-start | bytes 728 | tf_op jit(solution)/shard_map/ppermute | solution.py:19
  437.2 8.1 %collective-permute-start.118 = (f32[18,10,1]{2,0,1:T(8,128)S(1)}, f32[18,10,1]{2,0,1:T(8,128)S(1)}, u32[]{:S(2)}, u32[]{:S(2)}) collective-permute-start(f32[18,10,1]{2,0,1:T(8,128)S(1)} %get-tuple-element.42), channel_id=1, source_target_pairs={{1,0},{3,2},{5,4},{7,6},{9,8},{11,10},{13,12},{15,14},{17,16},{19,... | collective-permute-start | bytes 2168 | tf_op jit(solution)/shard_map/ppermute | solution.py:21
  438.5 7.9 %collective-permute-start.119 = (f32[18,10,1]{2,0,1:T(8,128)S(1)}, f32[18,10,1]{2,0,1:T(8,128)S(1)}, u32[]{:S(2)}, u32[]{:S(2)}) collective-permute-start(f32[18,10,1]{2,0,1:T(8,128)S(1)} %get-tuple-element.43), channel_id=1, source_target_pairs={{0,1},{2,3},{4,5},{6,7},{8,9},{10,11},{12,13},{14,15},{16,17},{18,... | collective-permute-start | bytes 2168 | tf_op jit(solution)/shard_map/ppermute | solution.py:19
  460.3 8.0 %collective-permute-start.124 = (f32[18,10,1]{2,0,1:T(8,128)S(1)}, f32[18,10,1]{2,0,1:T(8,128)S(1)}, u32[]{:S(2)}, u32[]{:S(2)}) collective-permute-start(f32[18,10,1]{2,0,1:T(8,128)S(1)} %get-tuple-element.38), channel_id=1, source_target_pairs={{1,0},{3,2},{5,4},{7,6},{9,8},{11,10},{13,12},{15,14},{17,16},{19,... | collective-permute-start | bytes 2168 | tf_op jit(solution)/shard_map/ppermute | solution.py:21
  461.6 8.0 %collective-permute-start.125 = (f32[18,10,1]{2,0,1:T(8,128)S(1)}, f32[18,10,1]{2,0,1:T(8,128)S(1)}, u32[]{:S(2)}, u32[]{:S(2)}) collective-permute-start(f32[18,10,1]{2,0,1:T(8,128)S(1)} %get-tuple-element.39), channel_id=1, source_target_pairs={{0,1},{2,3},{4,5},{6,7},{8,9},{10,11},{12,13},{14,15},{16,17},{18,... | collective-permute-start | bytes 2168 | tf_op jit(solution)/shard_map/ppermute | solution.py:19
  483.3 8.0 %collective-permute-start.130 = (f32[18,10,1]{2,0,1:T(8,128)S(1)}, f32[18,10,1]{2,0,1:T(8,128)S(1)}, u32[]{:S(2)}, u32[]{:S(2)}) collective-permute-start(f32[18,10,1]{2,0,1:T(8,128)S(1)} %get-tuple-element.34), channel_id=1, source_target_pairs={{1,0},{3,2},{5,4},{7,6},{9,8},{11,10},{13,12},{15,14},{17,16},{19,... | collective-permute-start | bytes 2168 | tf_op jit(solution)/shard_map/ppermute | solution.py:21
  484.6 8.0 %collective-permute-start.131 = (f32[18,10,1]{2,0,1:T(8,128)S(1)}, f32[18,10,1]{2,0,1:T(8,128)S(1)}, u32[]{:S(2)}, u32[]{:S(2)}) collective-permute-start(f32[18,10,1]{2,0,1:T(8,128)S(1)} %get-tuple-element.35), channel_id=1, source_target_pairs={{0,1},{2,3},{4,5},{6,7},{8,9},{10,11},{12,13},{14,15},{16,17},{18,... | collective-permute-start | bytes 2168 | tf_op jit(solution)/shard_map/ppermute | solution.py:19
  (87 other events, 486.4 us)
where the time goes:
time: 497 us; the launch traced here: 493 us
  starting transfers between devices  297 us (60%)
  waiting for transfers between devices  166 us (33%)
  local copies, waits for them, and re-layouts  16.8 us (3%)
  other arithmetic  10.4 us (2%)
    ppermute x66, starting transfers between devices, extended(): lax.ppermute(tail, axis, [(i, (i + 1) % count) for i in range(ends)])  212 us
    ppermute x66, waiting for transfers between devices, extended(): lax.ppermute(head, axis, [((i + 1) % count, i) for i in range(ends)])  135 us
    ppermute x66, starting transfers between devices, extended(): lax.ppermute(head, axis, [((i + 1) % count, i) for i in range(ends)])  85.1 us
    ppermute x66, waiting for transfers between devices, extended(): lax.ppermute(tail, axis, [(i, (i + 1) % count) for i in range(ends)])  30.7 us
    reshape x3, local copies, waits for them, and re-layouts, mean_cells(): field.reshape(n // 2, 2, m // 2, 2, k // 2, 2).sum(axis=(1, 3, 5)) * 0.125  12.4 us
  transfers between devices with their start and end apart: 132, of which 66 were waited for; matrix products, arithmetic and copies ran while one was open for 4% of the time, Pallas kernels for 0%

commit v1 on v0

v1 whole, which is shorter than its diff:
```python
import functools

import jax
import jax.numpy as jnp
from jax import lax
from jax.experimental import pallas as pl
from jax.experimental.pallas import tpu as pltpu
from jax.sharding import PartitionSpec as P

COARSE_DEGREE = 6
AXES = ("gx", "gy", "gz")
LANES = 128
TILE = 8
MESH = pl.DeviceIdType.MESH
F32 = jnp.float32


def div(a, n):
    if n & (n - 1) == 0:
        return lax.shift_right_logical(a, jnp.int32(n.bit_length() - 1))
    return a // n


def mod(a, n):
    if n & (n - 1) == 0:
        return a & jnp.int32(n - 1)
    return a % n


def iota(shape, dim):
    return lax.broadcasted_iota(jnp.int32, shape, dim)


def dot(a, b):
    return lax.dot(a, b, precision=lax.Precision.HIGHEST, preferred_element_type=F32)


def up8(n):
    return -(-n // TILE) * TILE


def upl(n):
    return -(-n // LANES) * LANES


def restrict(v, dims, width_out, offset):
    x, y, z = dims
    rows, cols = (x // 2) * (y // 2), x * y
    r, s = iota((rows, cols), 0), iota((rows, cols), 1)
    hit = (div(div(s, y), 2) == div(r, y // 2)) & (div(mod(s, y), 2) == mod(r, y // 2))
    left = jnp.where(hit, 0.125, 0.0).astype(F32)
    k, l = iota((v.shape[1], width_out), 0), iota((v.shape[1], width_out), 1)
    right = jnp.where((l == div(k, 2) + offset) & (k < z), 1.0, 0.0).astype(F32)
    return dot(dot(left, v), right)


def prolong(e, dims, width_out, coarse_y, x0, y0, z0):
    x, y, z = dims
    rows, cols = x * y, e.shape[0]
    r, s = iota((rows, cols), 0), iota((rows, cols), 1)
    want = (div(div(r, y), 2) + x0) * coarse_y + div(mod(r, y), 2) + y0
    left = jnp.where(s == want, 1.0, 0.0).astype(F32)
    k, l = iota((e.shape[1], width_out), 0), iota((e.shape[1], width_out), 1)
    right = jnp.where((k == div(l, 2) + z0) & (l < z), 1.0, 0.0).astype(F32)
    return dot(dot(left, e), right)


def harmonic(a, b):
    return 2.0 * a * b / (a + b)


def make_coefs(c, around, edges, scale):
    links, total = [], None
    for near, edge in zip(around, edges):
        face = harmonic(c, jnp.where(edge, c, near))
        total = face if total is None else total + face
        links.append(jnp.where(edge, 0.0, face) * scale)
    total = total * scale
    return links, total, 1.0 / total


def apply_op(v, around, coefs):
    links, total, unused = coefs
    out = total * v
    for near, link in zip(around, links):
        out = out - link * near
    return out


def chebyshev(start, source, steps, lower, upper, coefs, near_of):
    theta = (upper + lower) / 2.0
    delta = (upper - lower) / 2.0
    sigma = theta / delta
    rho_now = 1.0 / sigma
    inv = coefs[2]
    if start is None:
        update = source * inv * (1.0 / theta)
        field = update
    else:
        remain = source - apply_op(start, near_of(start), coefs)
        update = remain * inv * (1.0 / theta)
        field = start + update
    for index in range(steps - 1):
        rho_next = 1.0 / (2.0 * sigma - rho_now)
        remain = source - apply_op(field, near_of(field), coefs)
        update = rho_next * rho_now * update + (2.0 * rho_next / delta) * (remain * inv)
        field = field + update
        rho_now = rho_next
    return field


def kernel(sizes, dims0, b_ref, c_ref, p_ref, q_ref, *scratch):
    (v0, ys0, zs0, xr0, yr0, zr0, ey0, v1, ys1, zs1, xr1, yr1, zr1, ey1, tile, slots,
     send0, recv0, send1, recv1, gsend, grecv) = scratch
    pos = tuple(lax.axis_index(a) for a in AXES)
    dims1 = tuple(d // 2 for d in dims0)
    dims2 = tuple(d // 2 for d in dims1)
    whole2 = tuple(d * n for d, n in zip(dims2, sizes))
    whole3 = tuple(d // 2 for d in whole2)
    nx, ny, nz = sizes
    count = nx * ny * nz
    me = (pos[0] * ny + pos[1]) * nz + pos[2]
    width2, width3 = upl(whole2[2]), upl(whole3[2])

    def coords(index):
        return (index // (ny * nz), (index // nz) % ny, index % nz)

    barrier = pltpu.get_barrier_semaphore()

    def greet(step, unused):
        pl.semaphore_signal(barrier, inc=1, device_id=coords((me + step) % count), device_id_type=MESH)
        return unused

    for ref in (xr0, yr0, zr0, xr1, yr1, zr1, ey0, ey1):
        ref[...] = jnp.zeros_like(ref)
    lax.fori_loop(1, count, greet, 0)

    def exists(axis, side):
        return pos[axis] > 0 if side == 0 else pos[axis] < sizes[axis] - 1

    def peer(axis, side):
        return tuple(p + ((-1, 1)[side] if a == axis else 0) for a, p in enumerate(pos))

    def copies(level, slot):
        x, y, z = (dims0, dims1)[level]
        rows = x * y
        v, ys, zs, xr, yr, zr, send, recv = (
            (v0, ys0, zs0, xr0, yr0, zr0, send0, recv0),
            (v1, ys1, zs1, xr1, yr1, zr1, send1, recv1),
        )[level]
        edge = up8(y)
        for axis in range(3):
            for side in range(2):
                if axis == 0:
                    start = 0 if side == 0 else rows - edge
                    src, dst = v.at[slot, pl.ds(start, edge)], xr.at[slot, 1 - side]
                elif axis == 1:
                    src, dst = ys.at[slot, side], yr.at[slot, 1 - side]
                else:
                    src, dst = zs.at[slot, side], zr.at[slot, 1 - side]
                yield axis, side, pltpu.make_async_remote_copy(
                    src_ref=src, dst_ref=dst,
                    send_sem=send.at[slot, 2 * axis + side],
                    recv_sem=recv.at[slot, 2 * axis + 1 - side],
                    device_id=peer(axis, side), device_id_type=MESH,
                )

    def post(level, slot, value):
        x, y, z = (dims0, dims1)[level]
        rows = x * y
        v, ys, zs = ((v0, ys0, zs0), (v1, ys1, zs1))[level]
        v[slot] = value
        for side in range(2):
            ys[slot, side] = v[slot, pl.ds(0 if side == 0 else y - 1, x, stride=y), :]
            lane = iota((TILE, LANES), 1)
            packed = jnp.zeros((TILE, LANES), F32)
            for t in range(rows // TILE):
                part = value[t * TILE:(t + 1) * TILE]
                shift = (t if side == 0 else t - (z - 1)) % LANES
                if shift:
                    part = pltpu.roll(part, shift, 1)
                packed = jnp.where(lane == t, part, packed)
            zs[slot, side] = packed
        for axis, side, copy in copies(level, slot):
            @pl.when(exists(axis, side))
            def _():
                copy.start()

    def drain(level, slot):
        for axis, side, copy in copies(level, slot):
            @pl.when(exists(axis, side))
            def _():
                copy.wait_send()

    def collect(level, slot, value):
        x, y, z = (dims0, dims1)[level]
        rows = x * y
        xr, yr, zr, ey, recv = ((xr0, yr0, zr0, ey0, recv0), (xr1, yr1, zr1, ey1, recv1))[level]
        for axis in range(3):
            for side in range(2):
                dst = (xr, yr, zr)[axis].at[slot, side]
                @pl.when(exists(axis, side))
                def _():
                    pltpu.make_async_copy(dst, dst, recv.at[slot, 2 * axis + side]).wait()
        edge = up8(y)
        below = jnp.concatenate([xr[slot, 0], value], 0)[edge - y:edge - y + rows]
        above = jnp.concatenate([value, xr[slot, 1]], 0)[y:y + rows]
        ey[slot, 0, pl.ds(0, x, stride=y), :] = yr[slot, 0]
        ey[slot, 1, pl.ds(y - 1, x, stride=y), :] = yr[slot, 1]
        row = mod(iota((rows, LANES), 0), y)
        lane = iota((rows, LANES), 1)
        left = jnp.where(row == 0, ey[slot, 0], pltpu.roll(value, 1, 0))
        right = jnp.where(row == y - 1, ey[slot, 1], pltpu.roll(value, rows - 1, 0))

        def unpack(part, place):
            out = []
            for t in range(rows // TILE):
                shift = (place - t) % LANES
                out.append(pltpu.roll(part, shift, 1) if shift else part)
            return jnp.concatenate(out, 0)

        front = jnp.where(lane == 0, unpack(zr[slot, 0], 0), pltpu.roll(value, 1, 1))
        back = jnp.where(lane == z - 1, unpack(zr[slot, 1], z - 1), pltpu.roll(value, LANES - 1, 1))
        return (below, above, left, right, front, back)

    def local_edges(dims):
        x, y, z = dims
        rows = x * y
        plane, row, lane = div(iota((rows, LANES), 0), y), mod(iota((rows, LANES), 0), y), iota((rows, LANES), 1)
        return tuple(
            index + pos[axis] * dims[axis] == (0 if side == 0 else dims[axis] * sizes[axis] - 1)
            for axis, index in enumerate((plane, row, lane)) for side in range(2)
        )

    def whole_edges(dims, shape):
        x, y, z = dims
        plane, row, lane = div(iota(shape, 0), y), mod(iota(shape, 0), y), iota(shape, 1)
        return (plane == 0, plane == x - 1, row == 0, row == y - 1, lane == 0, lane >= z - 1)

    def whole_near(dims):
        x, y, z = dims
        rows = x * y

        def near(v):
            return (
                pltpu.roll(v, y, 0), pltpu.roll(v, rows - y, 0),
                pltpu.roll(v, 1, 0), pltpu.roll(v, rows - 1, 0),
                pltpu.roll(v, 1, 1), pltpu.roll(v, v.shape[1] - 1, 1),
            )
        return near

    def gather_copy(kind, step):
        target = coords((me + step) % count)
        return pltpu.make_async_remote_copy(
            src_ref=tile.at[kind], dst_ref=slots.at[kind, me],
            send_sem=gsend.at[kind], recv_sem=grecv.at[kind],
            device_id=target, device_id_type=MESH,
        )

    def gather_start(kind, value):
        tile[kind] = value

        def go(step, unused):
            gather_copy(kind, step).start()
            return unused
        lax.fori_loop(1, count, go, 0)

    def gather_finish(kind):
        part = slots.at[kind, pl.ds(0, count - 1)]
        pltpu.make_async_copy(part, part, grecv.at[kind]).wait()
        slots[kind, me] = tile[kind]
        per = LANES // dims2[2]
        block = dims2[0] * dims2[1]
        columns = []
        for lane_tile in range(width2 // LANES):
            rows = []
            for gx in range(nx):
                for gy in range(ny):
                    total = None
                    for gz in range(lane_tile * per, min((lane_tile + 1) * per, nz)):
                        part = slots[kind, (gx * ny + gy) * nz + gz]
                        total = part if total is None else total + part
                    rows.append(total)
            columns.append(jnp.concatenate(rows, 0))
        stacked = columns[0] if len(columns) == 1 else jnp.concatenate(columns, 1)
        n = whole2[0] * whole2[1]
        r, s = iota((n, n), 0), iota((n, n), 1)
        X, Y = div(r, whole2[1]), mod(r, whole2[1])
        want = (div(X, dims2[0]) * ny + div(Y, dims2[1])) * block + mod(X, dims2[0]) * dims2[1] + mod(Y, dims2[1])
        return dot(jnp.where(s == want, 1.0, 0.0).astype(F32), stacked)

    offset = (pos[2] % (LANES // dims2[2])) * dims2[2]

    def fill(c, dims):
        return jnp.where(iota(c.shape, 1) < dims[2], c, 1.0)

    c0 = c_ref[...].reshape(dims0[0] * dims0[1], LANES)
    b0 = b_ref[...].reshape(dims0[0] * dims0[1], LANES)
    c1 = restrict(c0, dims0, LANES, 0)
    c2_own = restrict(c1, dims1, LANES, offset)
    c1 = fill(c1, dims1)
    pl.semaphore_wait(barrier, count - 1)

    post(0, 0, c0)
    post(1, 0, c1)
    gather_start(0, c2_own)

    coefs0 = make_coefs(c0, collect(0, 0, c0), local_edges(dims0), 1.0)

    def near_at(level, slots_used):
        queue = list(slots_used)

        def near(v):
            slot = queue.pop(0)
            post(level, slot, v)
            return collect(level, slot, v)
        return near

    near0 = near_at(0, range(1, 6))
    x0 = chebyshev(None, b0, 2, 0.3, 2.0, coefs0, near0)
    r0 = b0 - apply_op(x0, near0(x0), coefs0)
    b1 = restrict(r0, dims0, LANES, 0)

    coefs1 = make_coefs(c1, collect(1, 0, c1), local_edges(dims1), 0.25)
    near1 = near_at(1, range(1, 5))
    x1 = chebyshev(None, b1, 2, 0.3, 2.0, coefs1, near1)
    r1 = b1 - apply_op(x1, near1(x1), coefs1)
    gather_start(1, restrict(r1, dims1, LANES, offset))

    c2 = gather_finish(0)
    shape2 = (whole2[0] * whole2[1], width2)
    near2 = whole_near(whole2)
    c3 = fill(restrict(c2, whole2, width3, 0), whole3)
    c2 = fill(c2, whole2)
    coefs2 = make_coefs(c2, near2(c2), whole_edges(whole2, shape2), 0.25 ** 2)
    near3 = whole_near(whole3)
    coefs3 = make_coefs(c3, near3(c3), whole_edges(whole3, c3.shape), 0.25 ** 3)

    b2 = gather_finish(1)
    x2 = chebyshev(None, b2, 2, 0.3, 2.0, coefs2, near2)
    r2 = b2 - apply_op(x2, near2(x2), coefs2)
    b3 = restrict(r2, whole2, width3, 0)
    x3 = chebyshev(None, b3, COARSE_DEGREE, 0.05, 2.0, coefs3, near3)
    x2 = x2 + prolong(x3, whole2, width2, whole3[1], 0, 0, 0)
    x2 = chebyshev(x2, b2, 2, 0.3, 2.0, coefs2, near2)

    x1 = x1 + prolong(x2, dims1, LANES, whole2[1], pos[0] * dims2[0], pos[1] * dims2[1], pos[2] * dims2[2])
    x1 = chebyshev(x1, b1, 2, 0.3, 2.0, coefs1, near1)
    x0 = x0 + prolong(x1, dims0, LANES, dims1[1], 0, 0, 0)
    x0 = chebyshev(x0, b0, 2, 0.3, 2.0, coefs0, near0)
    p_ref[...] = x0.reshape(p_ref.shape)
    res = b0 - apply_op(x0, near0(x0), coefs0)
    q_ref[...] = res.reshape(q_ref.shape)

    for slot in range(6):
        drain(0, slot)
    for slot in range(5):
        drain(1, slot)
    for kind in range(2):
        part = slots.at[kind, pl.ds(0, count - 1)]
        pltpu.make_async_copy(part, part, gsend.at[kind]).wait()


def solution(mesh):
    sizes = tuple(mesh.shape[a] for a in AXES)
    count = sizes[0] * sizes[1] * sizes[2]

    def per_device(b, c):
        dims0 = b.shape
        scratch = []
        for slots, (x, y, z) in ((6, dims0), (5, tuple(d // 2 for d in dims0))):
            scratch += [
                pltpu.VMEM((slots, x * y, LANES), F32),
                pltpu.VMEM((slots, 2, x, LANES), F32),
                pltpu.VMEM((slots, 2, TILE, LANES), F32),
                pltpu.VMEM((slots, 2, up8(y), LANES), F32),
                pltpu.VMEM((slots, 2, x, LANES), F32),
                pltpu.VMEM((slots, 2, TILE, LANES), F32),
                pltpu.VMEM((slots, 2, x * y, LANES), F32),
            ]
        scratch += [
            pltpu.VMEM((2, TILE, LANES), F32),
            pltpu.VMEM((2, count, TILE, LANES), F32),
            pltpu.SemaphoreType.DMA((6, 6)), pltpu.SemaphoreType.DMA((6, 6)),
            pltpu.SemaphoreType.DMA((5, 6)), pltpu.SemaphoreType.DMA((5, 6)),
            pltpu.SemaphoreType.DMA((2,)), pltpu.SemaphoreType.DMA((2,)),
        ]
        shape = jax.ShapeDtypeStruct(dims0, F32)
        return pl.pallas_call(
            functools.partial(kernel, sizes, dims0),
            out_shape=(shape, shape),
            in_specs=[pl.BlockSpec(memory_space=pltpu.VMEM)] * 2,
            out_specs=(pl.BlockSpec(memory_space=pltpu.VMEM),) * 2,
            scratch_shapes=scratch,
            compiler_params=pltpu.CompilerParams(collective_id=0, has_side_effects=True),
        )(b, c)

    spec = P(*AXES)
    return jax.shard_map(per_device, mesh=mesh, in_specs=(spec, spec), out_specs=(spec, spec), check_vma=False)
```

time: 497 us -> 50.3 us (0.10)
  starting transfers between devices: 297 us -> 0 us
  waiting for transfers between devices: 166 us -> 0 us
  Pallas kernels: 0 us -> 47.3 us
  local copies, waits for them, and re-layouts: 16.8 us -> 2.14 us
  other arithmetic: 10.4 us -> 0 us
    ppermute x132 -> x0, starting transfers between devices: 297 us -> none  [the longest x66 212 us: extended(): lax.ppermute(tail, axis, [(i, (i + 1) % count) for i in range(ends)])]
    ppermute x132 -> x0, waiting for transfers between devices: 166 us -> none  [the longest x66 135 us: extended(): lax.ppermute(head, axis, [((i + 1) % count, i) for i in range(ends)])]
    pallas_call x0 -> x1, Pallas kernels: none -> 47.3 us  [per_device(): pl.pallas_call(functools.partial(kernel, sizes, dims0), out_shape=(shape,...]
    reshape x7 -> x0, local copies, waits for them, and re-layouts: 12.9 us -> none  [the longest x3 12.4 us: mean_cells(): field.reshape(n // 2, 2, m // 2, 2, k // 2, 2).sum(axis=(1, 3, 5)) * 0.125]
    reduce_sum x8 -> x0, other arithmetic: 5.67 us -> none  [mean_cells(): field.reshape(n // 2, 2, m // 2, 2, k // 2, 2).sum(axis=(1, 3, 5)) * 0.125]
  transfers between devices with their start and end apart: 132 -> 0, of which waited for: 66 -> 0; matrix products, arithmetic and copies ran while one was open for 4% -> 0% of each run, Pallas kernels for 0% -> 0%
where the time goes in v1:
time: 50.3 us; the launch traced here: 50.1 us
  Pallas kernels  47.3 us (94%)
  local copies, waits for them, and re-layouts  2.14 us (4%)
  between operations  0.65 us (1%)
    pallas_call x1, Pallas kernels, per_device(): pl.pallas_call(functools.partial(kernel, sizes, dims0), out_shape=(shape,...  47.3 us
    unnamed x4, local copies, waits for them, and re-layouts  2.14 us

profile of v1, /device:TPU:0, one launch (start us, length us, event | category | flops | bytes accessed | tf_op | source)
XLA Modules:
  0.0 50.1 jit_solution(13257790907477687557)
XLA Ops:
  0.6 47.3 %shard_map.41 = (f32[16,8,128]{2,1,0:T(8,128)}, f32[16,8,128]{2,1,0:T(8,128)}) custom-call(f32[16,8,128]{2,1,0:T(8,128)} %b_ref.1, f32[16,8,128]{2,1,0:T(8,128)} %c_ref.1), custom_call_target="tpu_custom_call" | custom-call | tf_op jit(solution)/shard_map/pallas_call | solution.py:389
  48.0 0.0 copy-start
  48.0 1.5 %copy.6 = f32[16,8,128]{2,1,0:T(8,128)} copy(f32[16,8,128]{2,1,0:T(8,128)} %get-tuple-element.4) | data formatting | bytes 131072
  49.5 0.0 copy-done
  49.5 0.6 %copy.7 = f32[16,8,128]{2,1,0:T(8,128)} copy(f32[16,8,128]{2,1,0:T(8,128)S(1)} %copy-done) | data formatting | bytes 131072
Async XLA Ops:
  48.0 1.5 %copy-start = (f32[16,8,128]{2,1,0:T(8,128)S(1)}, f32[16,8,128]{2,1,0:T(8,128)}, u32[]{:S(2)}) copy-start(f32[16,8,128]{2,1,0:T(8,128)} %get-tuple-element.5) | copy-start | bytes 196612

commit v2 on v1

--- a/solution.py
+++ b/solution.py
@@ -65,6 +65,21 @@
     return dot(dot(left, e), right)
 
 
+def prolong_near(dims, rows_in, width_in, coarse_y, x0, y0, z0):
+    x, y, z = dims
+    shape = (x * y, rows_in)
+    i, j, s = div(iota(shape, 0), y), mod(iota(shape, 0), y), iota(shape, 1)
+    lefts = []
+    for sx, sy in ((0, 0), (-1, 0), (1, 0), (0, -1), (0, 1)):
+        want = (div(i + (sx + 2), 2) + (x0 - 1)) * coarse_y + div(j + (sy + 2), 2) + (y0 - 1)
+        lefts.append(jnp.where(s == want, 1.0, 0.0).astype(F32))
+    k, l = iota((width_in, LANES), 0), iota((width_in, LANES), 1)
+    rights = [
+        jnp.where((k == div(l + (sz + 2), 2) + (z0 - 1)) & (l < z), 1.0, 0.0).astype(F32) for sz in (0, -1, 1)
+    ]
+    return jnp.concatenate(lefts, 0), rights
+
+
 def harmonic(a, b):
     return 2.0 * a * b / (a + b)
 
@@ -87,22 +102,21 @@
     return out
 
 
-def chebyshev(start, source, steps, lower, upper, coefs, near_of):
+def chebyshev(start, source, steps, lower, upper, inv, op_of):
     theta = (upper + lower) / 2.0
     delta = (upper - lower) / 2.0
     sigma = theta / delta
     rho_now = 1.0 / sigma
-    inv = coefs[2]
     if start is None:
         update = source * inv * (1.0 / theta)
         field = update
     else:
-        remain = source - apply_op(start, near_of(start), coefs)
+        remain = source - op_of(start)
         update = remain * inv * (1.0 / theta)
         field = start + update
     for index in range(steps - 1):
         rho_next = 1.0 / (2.0 * sigma - rho_now)
-        remain = source - apply_op(field, near_of(field), coefs)
+        remain = source - op_of(field)
         update = rho_next * rho_now * update + (2.0 * rho_next / delta) * (remain * inv)
         field = field + update
         rho_now = rho_next
@@ -192,16 +206,27 @@
             def _():
                 copy.wait_send()
 
-    def collect(level, slot, value):
-        x, y, z = (dims0, dims1)[level]
-        rows = x * y
-        xr, yr, zr, ey, recv = ((xr0, yr0, zr0, ey0, recv0), (xr1, yr1, zr1, ey1, recv1))[level]
+    def arrive(level, slot):
+        xr, yr, zr, recv = ((xr0, yr0, zr0, recv0), (xr1, yr1, zr1, recv1))[level]
         for axis in range(3):
             for side in range(2):
                 dst = (xr, yr, zr)[axis].at[slot, side]
                 @pl.when(exists(axis, side))
                 def _():
                     pltpu.make_async_copy(dst, dst, recv.at[slot, 2 * axis + side]).wait()
+
+    def unpack(part, place, rows):
+        out = []
+        for t in range(rows // TILE):
+            shift = (place - t) % LANES
+            out.append(pltpu.roll(part, shift, 1) if shift else part)
+        return jnp.concatenate(out, 0)
+
+    def collect(level, slot, value):
+        arrive(level, slot)
+        x, y, z = (dims0, dims1)[level]
+        rows = x * y
+        xr, yr, zr, ey = ((xr0, yr0, zr0, ey0), (xr1, yr1, zr1, ey1))[level]
         edge = up8(y)
         below = jnp.concatenate([xr[slot, 0], value], 0)[edge - y:edge - y + rows]
         above = jnp.concatenate([value, xr[slot, 1]], 0)[y:y + rows]
@@ -212,15 +237,8 @@
         left = jnp.where(row == 0, ey[slot, 0], pltpu.roll(value, 1, 0))
         right = jnp.where(row == y - 1, ey[slot, 1], pltpu.roll(value, rows - 1, 0))
 
-        def unpack(part, place):
-            out = []
-            for t in range(rows // TILE):
-                shift = (place - t) % LANES
-                out.append(pltpu.roll(part, shift, 1) if shift else part)
-            return jnp.concatenate(out, 0)
-
-        front = jnp.where(lane == 0, unpack(zr[slot, 0], 0), pltpu.roll(value, 1, 1))
-        back = jnp.where(lane == z - 1, unpack(zr[slot, 1], z - 1), pltpu.roll(value, LANES - 1, 1))
+        front = jnp.where(lane == 0, unpack(zr[slot, 0], 0, rows), pltpu.roll(value, 1, 1))
+        back = jnp.where(lane == z - 1, unpack(zr[slot, 1], z - 1, rows), pltpu.roll(value, LANES - 1, 1))
         return (below, above, left, right, front, back)
 
     def local_edges(dims):
@@ -305,56 +323,113 @@
     post(1, 0, c1)
     gather_start(0, c2_own)
 
-    coefs0 = make_coefs(c0, collect(0, 0, c0), local_edges(dims0), 1.0)
-
-    def near_at(level, slots_used):
-        queue = list(slots_used)
-
-        def near(v):
-            slot = queue.pop(0)
-            post(level, slot, v)
-            return collect(level, slot, v)
-        return near
-
-    near0 = near_at(0, range(1, 6))
-    x0 = chebyshev(None, b0, 2, 0.3, 2.0, coefs0, near0)
-    r0 = b0 - apply_op(x0, near0(x0), coefs0)
+    lane0, row0, plane0 = (iota((dims0[0] * dims0[1], LANES), 1), mod(iota((dims0[0] * dims0[1], LANES), 0), dims0[1]),
+                           div(iota((dims0[0] * dims0[1], LANES), 0), dims0[1]))
+    sides0 = (plane0 == 0, plane0 == dims0[0] - 1, row0 == 0, row0 == dims0[1] - 1, lane0 == 0, lane0 == dims0[2] - 1)
+    near0 = whole_near(dims0)
+    near2, near3 = whole_near(whole2), whole_near(whole3)
+    rows0, edge0 = dims0[0] * dims0[1], dims0[1]
+    shape2 = (whole2[0] * whole2[1], width2)
+    store = {}
+
+    links0, total0, inv0 = make_coefs(c0, collect(0, 0, c0), local_edges(dims0), 1.0)
+    inner0 = [jnp.where(side, 0.0, link) for side, link in zip(sides0, links0)]
+    outer0 = [jnp.where(side, link, 0.0) for side, link in zip(sides0, links0)]
+
+    def op0(slot, filler=None):
+        def op(v):
+            post(0, slot, v)
+            out = apply_op(v, near0(v), (inner0, total0, None))
+            if filler is not None:
+                filler()
+            arrive(0, slot)
+            ey0[slot, 0, pl.ds(0, dims0[0], stride=edge0), :] = yr0[slot, 0]
+            ey0[slot, 1, pl.ds(edge0 - 1, dims0[0], stride=edge0), :] = yr0[slot, 1]
+            out = out - outer0[2] * ey0[slot, 0] - outer0[3] * ey0[slot, 1]
+            out = out - outer0[4] * unpack(zr0[slot, 0], 0, rows0)
+            out = out - outer0[5] * unpack(zr0[slot, 1], dims0[2] - 1, rows0)
+            return jnp.concatenate([
+                out[:edge0] - outer0[0][:edge0] * xr0[slot, 0],
+                out[edge0:rows0 - edge0],
+                out[rows0 - edge0:] - outer0[1][rows0 - edge0:] * xr0[slot, 1],
+            ], 0)
+        return op
+
+    def ops(*steps):
+        queue = list(steps)
+        return lambda v: queue.pop(0)(v)
+
+    def op1(slot, filler=None):
+        def op(v):
+            post(1, slot, v)
+            if filler is not None:
+                filler()
+            store["near1"] = collect(1, slot, v)
+            return apply_op(v, store["near1"], store["coefs1"])
+        return op
+
+    def fill_coefs1():
+        store["coefs1"] = make_coefs(c1, collect(1, 0, c1), local_edges(dims1), 0.25)
+
+    def fill_gather():
+        store["c2"] = gather_finish(0)
+
+    def fill_coefs2():
+        c2 = store["c2"]
+        store["c3"] = fill(restrict(c2, whole2, width3, 0), whole3)
+        c2 = fill(c2, whole2)
+        store["coefs2"] = make_coefs(c2, near2(c2), whole_edges(whole2, shape2), 0.25 ** 2)
+
+    def fill_coefs3():
+        c3 = store["c3"]
+        store["coefs3"] = make_coefs(c3, near3(c3), whole_edges(whole3, c3.shape), 0.25 ** 3)
+        store["prolong"] = prolong_near(
+            dims1, shape2[0], width2, whole2[1], pos[0] * dims2[0], pos[1] * dims2[1], pos[2] * dims2[2])
+
+    x0 = chebyshev(None, b0, 2, 0.3, 2.0, inv0, op0(1, fill_coefs1))
+    r0 = b0 - op0(2, fill_gather)(x0)
     b1 = restrict(r0, dims0, LANES, 0)
 
-    coefs1 = make_coefs(c1, collect(1, 0, c1), local_edges(dims1), 0.25)
-    near1 = near_at(1, range(1, 5))
-    x1 = chebyshev(None, b1, 2, 0.3, 2.0, coefs1, near1)
-    r1 = b1 - apply_op(x1, near1(x1), coefs1)
+    coefs1 = store["coefs1"]
+    x1 = chebyshev(None, b1, 2, 0.3, 2.0, coefs1[2], op1(1, fill_coefs2))
+    r1 = b1 - op1(2, fill_coefs3)(x1)
     gather_start(1, restrict(r1, dims1, LANES, offset))
-
-    c2 = gather_finish(0)
-    shape2 = (whole2[0] * whole2[1], width2)
-    near2 = whole_near(whole2)
-    c3 = fill(restrict(c2, whole2, width3, 0), whole3)
-    c2 = fill(c2, whole2)
-    coefs2 = make_coefs(c2, near2(c2), whole_edges(whole2, shape2), 0.25 ** 2)
-    near3 = whole_near(whole3)
-    coefs3 = make_coefs(c3, near3(c3), whole_edges(whole3, c3.shape), 0.25 ** 3)
+    coefs2, coefs3, left5, rights = store["coefs2"], store["coefs3"], *store["prolong"]
+
+    def op2(v):
+        return apply_op(v, near2(v), coefs2)
+
+    def op3(v):
+        return apply_op(v, near3(v), coefs3)
 
     b2 = gather_finish(1)
-    x2 = chebyshev(None, b2, 2, 0.3, 2.0, coefs2, near2)
-    r2 = b2 - apply_op(x2, near2(x2), coefs2)
+    x2 = chebyshev(None, b2, 2, 0.3, 2.0, coefs2[2], op2)
+    r2 = b2 - op2(x2)
     b3 = restrict(r2, whole2, width3, 0)
-    x3 = chebyshev(None, b3, COARSE_DEGREE, 0.05, 2.0, coefs3, near3)
+    x3 = chebyshev(None, b3, COARSE_DEGREE, 0.05, 2.0, coefs3[2], op3)
     x2 = x2 + prolong(x3, whole2, width2, whole3[1], 0, 0, 0)
-    x2 = chebyshev(x2, b2, 2, 0.3, 2.0, coefs2, near2)
-
-    x1 = x1 + prolong(x2, dims1, LANES, whole2[1], pos[0] * dims2[0], pos[1] * dims2[1], pos[2] * dims2[2])
-    x1 = chebyshev(x1, b1, 2, 0.3, 2.0, coefs1, near1)
+    x2 = chebyshev(x2, b2, 2, 0.3, 2.0, coefs2[2], op2)
+
+    rows1 = dims1[0] * dims1[1]
+    picked = dot(left5, x2)
+    spread = dot(picked, rights[0])
+    near_e = [spread[n * rows1:(n + 1) * rows1] for n in range(1, 5)] + [dot(picked[:rows1], m) for m in rights[1:]]
+    near_x = store["near1"]
+
+    def op1_known(v):
+        return apply_op(v, [a + b for a, b in zip(near_x, near_e)], coefs1)
+
+    x1 = x1 + spread[:rows1]
+    x1 = chebyshev(x1, b1, 2, 0.3, 2.0, coefs1[2], ops(op1_known, op1(3)))
     x0 = x0 + prolong(x1, dims0, LANES, dims1[1], 0, 0, 0)
-    x0 = chebyshev(x0, b0, 2, 0.3, 2.0, coefs0, near0)
+    x0 = chebyshev(x0, b0, 2, 0.3, 2.0, inv0, ops(op0(3), op0(4)))
     p_ref[...] = x0.reshape(p_ref.shape)
-    res = b0 - apply_op(x0, near0(x0), coefs0)
+    res = b0 - op0(5)(x0)
     q_ref[...] = res.reshape(q_ref.shape)
 
     for slot in range(6):
         drain(0, slot)
-    for slot in range(5):
+    for slot in range(4):
         drain(1, slot)
     for kind in range(2):
         part = slots.at[kind, pl.ds(0, count - 1)]
@@ -368,7 +443,7 @@
     def per_device(b, c):
         dims0 = b.shape
         scratch = []
-        for slots, (x, y, z) in ((6, dims0), (5, tuple(d // 2 for d in dims0))):
+        for slots, (x, y, z) in ((6, dims0), (4, tuple(d // 2 for d in dims0))):
             scratch += [
                 pltpu.VMEM((slots, x * y, LANES), F32),
                 pltpu.VMEM((slots, 2, x, LANES), F32),
@@ -382,7 +457,7 @@
             pltpu.VMEM((2, TILE, LANES), F32),
             pltpu.VMEM((2, count, TILE, LANES), F32),
             pltpu.SemaphoreType.DMA((6, 6)), pltpu.SemaphoreType.DMA((6, 6)),
-            pltpu.SemaphoreType.DMA((5, 6)), pltpu.SemaphoreType.DMA((5, 6)),
+            pltpu.SemaphoreType.DMA((4, 6)), pltpu.SemaphoreType.DMA((4, 6)),
             pltpu.SemaphoreType.DMA((2,)), pltpu.SemaphoreType.DMA((2,)),
         ]
         shape = jax.ShapeDtypeStruct(dims0, F32)

time: 50.3 us -> 47.3 us (0.940)
  Pallas kernels: 47.3 us -> 44.3 us
    pallas_call x1, Pallas kernels: 47.3 us -> 44.3 us  [per_device(): pl.pallas_call(functools.partial(kernel, sizes, dims0), out_shape=(shape,...]
where the time goes in v2:
time: 47.3 us; the launch traced here: 47.1 us
  Pallas kernels  44.3 us (94%)
  local copies, waits for them, and re-layouts  2.14 us (5%)
  between operations  0.65 us (1%)
    pallas_call x1, Pallas kernels, per_device(): pl.pallas_call(functools.partial(kernel, sizes, dims0), out_shape=(shape,...  44.3 us
    unnamed x4, local copies, waits for them, and re-layouts  2.14 us

profile of v2, /device:TPU:0, one launch (start us, length us, event | category | flops | bytes accessed | tf_op | source)
XLA Modules:
  0.0 47.1 jit_solution(157098499657277226)
XLA Ops:
  0.6 44.3 %shard_map.41 = (f32[16,8,128]{2,1,0:T(8,128)}, f32[16,8,128]{2,1,0:T(8,128)}) custom-call(f32[16,8,128]{2,1,0:T(8,128)} %b_ref.1, f32[16,8,128]{2,1,0:T(8,128)} %c_ref.1), custom_call_target="tpu_custom_call" | custom-call | tf_op jit(solution)/shard_map/pallas_call | solution.py:464
  45.0 0.0 copy-start
  45.0 1.5 %copy.6 = f32[16,8,128]{2,1,0:T(8,128)} copy(f32[16,8,128]{2,1,0:T(8,128)} %get-tuple-element.4) | data formatting | bytes 131072
  46.5 0.0 copy-done
  46.5 0.6 %copy.7 = f32[16,8,128]{2,1,0:T(8,128)} copy(f32[16,8,128]{2,1,0:T(8,128)S(1)} %copy-done) | data formatting | bytes 131072
Async XLA Ops:
  45.0 1.5 %copy-start = (f32[16,8,128]{2,1,0:T(8,128)S(1)}, f32[16,8,128]{2,1,0:T(8,128)}, u32[]{:S(2)}) copy-start(f32[16,8,128]{2,1,0:T(8,128)} %get-tuple-element.5) | copy-start | bytes 196612

commit v3 on v2

--- a/solution.py
+++ b/solution.py
@@ -31,8 +31,30 @@
     return lax.broadcasted_iota(jnp.int32, shape, dim)
 
 
-def dot(a, b):
-    return lax.dot(a, b, precision=lax.Precision.HIGHEST, preferred_element_type=F32)
+def parts(v):
+    high = v.astype(jnp.bfloat16)
+    rest = v - high.astype(F32)
+    middle = rest.astype(jnp.bfloat16)
+    return high, middle, (rest - middle.astype(F32)).astype(jnp.bfloat16)
+
+
+def pick_rows(left, v):
+    n = v.shape[1]
+    out = lax.dot(left, jnp.concatenate(parts(v), 1), preferred_element_type=F32)
+    return out[:, :n] + (out[:, n:2 * n] + out[:, 2 * n:])
+
+
+def pick_lanes(v, right):
+    n = v.shape[0]
+    if n % 16:
+        high, middle, low = (lax.dot(part, right, preferred_element_type=F32) for part in parts(v))
+        return high + (middle + low)
+    out = lax.dot(jnp.concatenate(parts(v), 0), right, preferred_element_type=F32)
+    return out[:n] + (out[n:2 * n] + out[2 * n:])
+
+
+def chosen(hit, value=1.0):
+    return jnp.where(hit, value, 0.0).astype(jnp.bfloat16)
 
 
 def up8(n):
@@ -48,10 +70,10 @@
     rows, cols = (x // 2) * (y // 2), x * y
     r, s = iota((rows, cols), 0), iota((rows, cols), 1)
     hit = (div(div(s, y), 2) == div(r, y // 2)) & (div(mod(s, y), 2) == mod(r, y // 2))
-    left = jnp.where(hit, 0.125, 0.0).astype(F32)
+    left = chosen(hit, 0.125)
     k, l = iota((v.shape[1], width_out), 0), iota((v.shape[1], width_out), 1)
-    right = jnp.where((l == div(k, 2) + offset) & (k < z), 1.0, 0.0).astype(F32)
-    return dot(dot(left, v), right)
+    right = chosen((l == div(k, 2) + offset) & (k < z))
+    return pick_lanes(pick_rows(left, v), right)
 
 
 def prolong(e, dims, width_out, coarse_y, x0, y0, z0):
@@ -59,10 +81,10 @@
     rows, cols = x * y, e.shape[0]
     r, s = iota((rows, cols), 0), iota((rows, cols), 1)
     want = (div(div(r, y), 2) + x0) * coarse_y + div(mod(r, y), 2) + y0
-    left = jnp.where(s == want, 1.0, 0.0).astype(F32)
+    left = chosen(s == want)
     k, l = iota((e.shape[1], width_out), 0), iota((e.shape[1], width_out), 1)
-    right = jnp.where((k == div(l, 2) + z0) & (l < z), 1.0, 0.0).astype(F32)
-    return dot(dot(left, e), right)
+    right = chosen((k == div(l, 2) + z0) & (l < z))
+    return pick_lanes(pick_rows(left, e), right)
 
 
 def prolong_near(dims, rows_in, width_in, coarse_y, x0, y0, z0):
@@ -72,10 +94,10 @@
     lefts = []
     for sx, sy in ((0, 0), (-1, 0), (1, 0), (0, -1), (0, 1)):
         want = (div(i + (sx + 2), 2) + (x0 - 1)) * coarse_y + div(j + (sy + 2), 2) + (y0 - 1)
-        lefts.append(jnp.where(s == want, 1.0, 0.0).astype(F32))
+        lefts.append(chosen(s == want))
     k, l = iota((width_in, LANES), 0), iota((width_in, LANES), 1)
     rights = [
-        jnp.where((k == div(l + (sz + 2), 2) + (z0 - 1)) & (l < z), 1.0, 0.0).astype(F32) for sz in (0, -1, 1)
+        chosen((k == div(l + (sz + 2), 2) + (z0 - 1)) & (l < z)) for sz in (0, -1, 1)
     ]
     return jnp.concatenate(lefts, 0), rights
 
@@ -179,14 +201,26 @@
                     device_id=peer(axis, side), device_id_type=MESH,
                 )
 
-    def post(level, slot, value):
+    def launch(level, slot, wanted):
+        for axis, side, copy in copies(level, slot):
+            if axis in wanted:
+                @pl.when(exists(axis, side))
+                def _():
+                    copy.start()
+
+    def post(level, slot, value, now=True):
         x, y, z = (dims0, dims1)[level]
         rows = x * y
         v, ys, zs = ((v0, ys0, zs0), (v1, ys1, zs1))[level]
         v[slot] = value
+        if now:
+            launch(level, slot, (0,))
         for side in range(2):
             ys[slot, side] = v[slot, pl.ds(0 if side == 0 else y - 1, x, stride=y), :]
-            lane = iota((TILE, LANES), 1)
+        if now:
+            launch(level, slot, (1,))
+        lane = iota((TILE, LANES), 1)
+        for side in range(2):
             packed = jnp.zeros((TILE, LANES), F32)
             for t in range(rows // TILE):
                 part = value[t * TILE:(t + 1) * TILE]
@@ -195,10 +229,8 @@
                     part = pltpu.roll(part, shift, 1)
                 packed = jnp.where(lane == t, part, packed)
             zs[slot, side] = packed
-        for axis, side, copy in copies(level, slot):
-            @pl.when(exists(axis, side))
-            def _():
-                copy.start()
+        if now:
+            launch(level, slot, (2,))
 
     def drain(level, slot):
         for axis, side, copy in copies(level, slot):
@@ -305,7 +337,7 @@
         r, s = iota((n, n), 0), iota((n, n), 1)
         X, Y = div(r, whole2[1]), mod(r, whole2[1])
         want = (div(X, dims2[0]) * ny + div(Y, dims2[1])) * block + mod(X, dims2[0]) * dims2[1] + mod(Y, dims2[1])
-        return dot(jnp.where(s == want, 1.0, 0.0).astype(F32), stacked)
+        return pick_rows(chosen(s == want), stacked)
 
     offset = (pos[2] % (LANES // dims2[2])) * dims2[2]
 
@@ -317,10 +349,12 @@
     c1 = restrict(c0, dims0, LANES, 0)
     c2_own = restrict(c1, dims1, LANES, offset)
     c1 = fill(c1, dims1)
+    post(0, 0, c0, False)
+    post(1, 0, c1, False)
     pl.semaphore_wait(barrier, count - 1)
 
-    post(0, 0, c0)
-    post(1, 0, c1)
+    launch(0, 0, (0, 1, 2))
+    launch(1, 0, (0, 1, 2))
     gather_start(0, c2_own)
 
     lane0, row0, plane0 = (iota((dims0[0] * dims0[1], LANES), 1), mod(iota((dims0[0] * dims0[1], LANES), 0), dims0[1]),
@@ -411,9 +445,9 @@
     x2 = chebyshev(x2, b2, 2, 0.3, 2.0, coefs2[2], op2)
 
     rows1 = dims1[0] * dims1[1]
-    picked = dot(left5, x2)
-    spread = dot(picked, rights[0])
-    near_e = [spread[n * rows1:(n + 1) * rows1] for n in range(1, 5)] + [dot(picked[:rows1], m) for m in rights[1:]]
+    picked = pick_rows(left5, x2)
+    spread = pick_lanes(picked, rights[0])
+    near_e = [spread[n * rows1:(n + 1) * rows1] for n in range(1, 5)] + [pick_lanes(picked[:rows1], m) for m in rights[1:]]
     near_x = store["near1"]
 
     def op1_known(v):

time: 47.3 us -> 46.1 us (0.975)
  Pallas kernels: 44.3 us -> 43.1 us
    pallas_call x1, Pallas kernels: 44.3 us -> 43.1 us  [per_device(): pl.pallas_call(functools.partial(kernel, sizes, dims0), out_shape=(shape,...]
where the time goes in v3:
time: 46.1 us; the launch traced here: 45.9 us
  Pallas kernels  43.1 us (93%)
  local copies, waits for them, and re-layouts  2.14 us (5%)
  between operations  0.65 us (1%)
    pallas_call x1, Pallas kernels, per_device(): pl.pallas_call(functools.partial(kernel, sizes, dims0), out_shape=(shape,...  43.1 us
    unnamed x4, local copies, waits for them, and re-layouts  2.14 us

profile of v3, /device:TPU:0, one launch (start us, length us, event | category | flops | bytes accessed | tf_op | source)
XLA Modules:
  0.0 45.9 jit_solution(10118562917404638400)
XLA Ops:
  0.6 43.1 %shard_map.41 = (f32[16,8,128]{2,1,0:T(8,128)}, f32[16,8,128]{2,1,0:T(8,128)}) custom-call(f32[16,8,128]{2,1,0:T(8,128)} %b_ref.1, f32[16,8,128]{2,1,0:T(8,128)} %c_ref.1), custom_call_target="tpu_custom_call" | custom-call | tf_op jit(solution)/shard_map/pallas_call | solution.py:498
  43.8 0.0 copy-start
  43.8 1.5 %copy.6 = f32[16,8,128]{2,1,0:T(8,128)} copy(f32[16,8,128]{2,1,0:T(8,128)} %get-tuple-element.4) | data formatting | bytes 131072
  45.3 0.0 copy-done
  45.3 0.6 %copy.7 = f32[16,8,128]{2,1,0:T(8,128)} copy(f32[16,8,128]{2,1,0:T(8,128)S(1)} %copy-done) | data formatting | bytes 131072
Async XLA Ops:
  43.8 1.5 %copy-start = (f32[16,8,128]{2,1,0:T(8,128)S(1)}, f32[16,8,128]{2,1,0:T(8,128)}, u32[]{:S(2)}) copy-start(f32[16,8,128]{2,1,0:T(8,128)} %get-tuple-element.5) | copy-start | bytes 196612
